TPU v7x, 128 devices: a whole 4x4x4 slice. The times are simulated.
128 devices in a mesh: rep: 32 (over x, z, core), layer: 4 (over y).
Axes of the slice: x: 4, y: 4, z: 4, core: 2. Of those that a mesh axis runs over, the one named last changes fastest.
Arguments:
- activations: bfloat16 [4, 16384, 8192], P('layer', 'rep'), may hold values from -6 to 6
- output_grads: bfloat16 [4, 16384, 8192], P('layer', 'rep'), may hold values from -6 to 6
- in_projection: bfloat16 [4, 32, 8192], P('layer'), may hold values from -0.0625 to 0.0625
- out_projection: bfloat16 [4, 32, 8192], P('layer'), may hold values from -0.0625 to 0.0625
- segment_ids: int32 [16384], P('rep'), may hold values from -1 to 61, as said below
- move_list: int32 [1984], P('rep'), may hold values from -1 to 1023, as said below
Outputs:
- factor: float32 [4, 1024, 1024], P('layer')
- features: bfloat16 [4, 1024, 1024], P('layer', 'rep')
- self_influence: float32 [1024], P('rep')
Inputs may be any that keep to these rules, and one draw needn't show every extreme that they name: `segment_ids`: within each replica's 512 tokens the values never fall; a run of equal values is one document; -1 marks tokens continuing the previous replica's last document and never occurs on replica 0; n documents start on a replica with values 0 to n - 1, n from 2 to 62, and some replica has exactly 62; all documents together are 1024; the last document ends at the end of the last replica. `move_list`: replica r's block of 62 entries gives for its documents in order of their first token (the one continuing onto replica r + 1 included) the destination row in 0 to 1023, and -1 past its last document; every row is named exactly once; the documents of replica r go to rows of replica r - 1, r or r + 1 (rows m * 32 to m * 32 + 31 belong to replica m).
All inputs are finite; a program needn't handle non-finite values.
Results may differ from a plain program's by a relative error of at most 0.0064.
Values may be sent and summed in bfloat16 or wider, within the bound.
A program may use at most 128 MiB of HBM per device.

v0:
```python
import jax
import jax.numpy as jnp
from jax import lax
from jax.sharding import PartitionSpec as P

BAL = 32
DAMPING = 0.05


def shifted(block, axis, distance):
    devices = range(lax.axis_size(axis))
    route = [(i - distance, i) for i in devices if i - distance in devices]
    return lax.ppermute(block, axis, route)


def on_device(activations, output_grads, in_projection, out_projection, segment_ids, move_list):
    contract = (((1,), (1,)), ((), ()))
    left = lax.dot_general(
        in_projection[0], activations[0], contract, preferred_element_type=jnp.float32
    ).astype(jnp.bfloat16)
    right = lax.dot_general(
        out_projection[0], output_grads[0], contract, preferred_element_type=jnp.float32
    ).astype(jnp.bfloat16)
    doc_slots = move_list.shape[0]
    width = left.shape[0] * right.shape[0]
    slot_ids = jnp.arange(doc_slots + 1, dtype=jnp.int32) - 1
    member = (segment_ids[None, :] == slot_ids[:, None]).astype(jnp.bfloat16)
    masked = member[:, None, :] * left[None, :, :]
    blocks = lax.dot_general(
        masked, right, (((2,), (1,)), ((), ())), preferred_element_type=jnp.float32
    )
    sums = blocks.reshape(doc_slots + 1, width)
    counts = jnp.sum(member.astype(jnp.float32), axis=1)
    carried_sum, carried_count = shifted((sums[:1], counts[:1]), "rep", -1)
    last_slot = jnp.max(segment_ids)
    takes = (slot_ids[1:] == last_slot).astype(jnp.float32)
    totals = sums[1:] + takes[:, None] * carried_sum
    lengths = counts[1:] + takes * carried_count[0]
    safe_len = jnp.maximum(lengths, 1.0)
    local_features = (totals / jnp.sqrt(safe_len)[:, None]).astype(jnp.bfloat16)
    replica = lax.axis_index("rep")
    n_rep = lax.axis_size("rep")
    offsets = jnp.where(move_list >= 0, move_list // BAL - replica, 5)
    within = move_list % BAL
    row_ids = jnp.arange(BAL, dtype=jnp.int32)

    def arrange(step_offset):
        select = ((offsets[None, :] == step_offset) & (within[None, :] == row_ids[:, None])).astype(
            jnp.bfloat16
        )
        return jnp.dot(select, local_features, preferred_element_type=jnp.float32).astype(
            jnp.bfloat16
        )

    staying = arrange(0)
    from_right = shifted(arrange(-1), "rep", -1)
    from_left = shifted(arrange(1), "rep", 1)
    mine = (
        staying.astype(jnp.float32) + from_right.astype(jnp.float32) + from_left.astype(jnp.float32)
    ).astype(jnp.bfloat16)
    rows_contract = (((0,), (0,)), ((), ()))
    local_gram = lax.dot_general(mine, mine, rows_contract, preferred_element_type=jnp.float32)
    gram = lax.psum(local_gram, "rep")
    total_docs = BAL * n_rep
    hessian = gram / total_docs + DAMPING * jnp.eye(width, dtype=jnp.float32)
    lower = jnp.linalg.cholesky(hessian)
    solved = lax.linalg.triangular_solve(
        lower, mine.T.astype(jnp.float32), left_side=True, lower=True
    )
    quad = jnp.sum(solved * solved, axis=0) / width
    influence = lax.psum(quad, "layer")
    return (lower.T[None], mine[None], influence)


def solution(mesh):
    placed = (
        P("layer", "rep", None),
        P("layer", "rep", None),
        P("layer", None, None),
        P("layer", None, None),
        P("rep"),
        P("rep"),
    )
    return jax.shard_map(
        on_device,
        mesh=mesh,
        in_specs=placed,
        out_specs=(P("layer", None, None), P("layer", "rep", None), P("rep")),
        check_vma=False,
    )
```

profile of v0, /device:TPU:6, one launch (start us, length us, event | category | flops | bytes accessed | tf_op | source)
XLA Modules:
  0.0 522.8 jit_solution(4648112741380501496)
XLA Ops:
  7.2 0.9 convert_reduce_fusion
  8.1 5.7 %collective-permute-start.1 = (f32[1]{0:T(128)S(1)}, f32[1]{0:T(128)}, u32[]{:S(2)}, u32[]{:S(2)}) collective-permute-start(f32[1]{0:T(128)S(1)} %bitcast.148), channel_id=1, source_target_pairs={{4,0},{8,4},{12,8},{16,12},{20,16},{24,20},{28,24},{32,28},{36,32}... | collective-permute-start | bytes 20 | tf_op jit(solution)/shard_map/ppermute | solution.py:13
  13.8 0.8 compare_convert_fusion
  14.6 6.2 %fusion.10 = bf16[32,512]{1,0:T(8,128)(2,1)S(1)} fusion(bf16[1,512,8192]{2,1,0:T(8,128)(2,1)} %param.6, bf16[1,32,8192]{2,1,0:T(8,128)(2,1)} %param.8), kind=kOutput, calls=%fused_computation.33 | convolution fusion | flops 268451840 | bytes 8945664 | tf_op jit(solution)/shard_map/dot_general | solution.py:18
  20.8 6.7 %fusion.7 = f32[63,32,32]{2,1,0:T(8,128)S(1)} fusion(bf16[32,512]{1,0:T(8,128)(2,1)S(1)} %fusion.10, bf16[63,512]{1,0:T(8,128)(2,1)S(1)} %compare_convert_fusion, bf16[1,512,8192]{2,1,0:T(8,128)(2,1)} %param.7, bf16[1,32,8192]{2,1,0:T(8,128)(2,1)S(1)} %copy-done), kind=kOutput, calls=%fused_computation.14 | convolution fusion | flops 335544320 | bytes 9268224 | tf_op jit(solution)/shard_map/dot_general | solution.py:29
  27.6 2.6 collective-permute-start
  32.3 1.4 maximum_sqrt_fusion
  34.1 1.9 collective-permute-start.3
  36.2 5.8 %collective-permute-start.2 = (bf16[32,1024]{1,0:T(8,128)(2,1)S(1)}, bf16[32,1024]{1,0:T(8,128)(2,1)S(1)}, u32[]{:S(2)}, u32[]{:S(2)}) collective-permute-start(bf16[32,1024]{1,0:T(8,128)(2,1)S(1)} %convolution_convert_fusion.1), channel_id=1, source_target_pairs={{4,0},{8,4},{12,8},{16,12},{20,16},{24,20},{28,24},{32,28},{36,32}... | collective-permute-start | bytes 196616 | tf_op jit(solution)/shard_map/ppermute | solution.py:13
  42.2 1.7 collective-permute-done.2
  43.9 2.8 fusion.102
  46.8 114.7 %all-reduce.3.cloned.1.call-done = f32[1024,1024]{0,1:T(8,128)} async-done(((f32[1024,1024]{0,1:T(8,128)}), f32[1024,1024]{0,1:T(8,128)}) %all-reduce.3.cloned.1.call-update) | async-done | bytes 4194320 | tf_op jit(solution)/shard_map/psum | solution.py:63
  161.5 5.1 select_add_fusion
  166.5 5.8 %copy.29 = f32[1024,1024]{1,0:T(8,128)} copy(f32[1024,1024]{0,1:T(8,128)} %select_add_fusion) | data formatting | bytes 8388608 | tf_op jit(solution)/shard_map/add | solution.py:65
  172.3 4.5 fusion.4
  176.8 2.0 copy-done.2
  178.8 11.7 %cholesky.222 = f32[128,128]{1,0:T(8,128)S(1)} custom-call(f32[128,128]{1,0:T(8,128)S(1)} %cholesky.577), custom_call_target="Cholesky" | custom-call | tf_op jit(solution)/shard_map/jit(cholesky)/cholesky | solution.py:66
  190.7 9.8 %custom-call.62 = f32[1,128,128]{1,2,0:T(8,128)S(1)} custom-call(f32[1,128,128]{2,1,0:T(8,128)S(1)} %get-tuple-element.48), custom_call_target="InvertDiagBlocksLowerTriangular" | custom-call | tf_op jit(solution)/shard_map/jit(cholesky)/cholesky | solution.py:66
  200.5 1.5 fusion.35
  202.2 1.6 convolution_subtract_fusion
  203.8 11.7 %cholesky.243 = f32[128,128]{1,0:T(8,128)S(1)} custom-call(f32[128,128]{1,0:T(8,128)S(1)} %cholesky.581), custom_call_target="Cholesky" | custom-call | tf_op jit(solution)/shard_map/jit(cholesky)/cholesky | solution.py:66
  215.8 9.8 %custom-call.63 = f32[1,128,128]{1,2,0:T(8,128)S(1)} custom-call(f32[1,128,128]{2,1,0:T(8,128)S(1)} %get-tuple-element.46), custom_call_target="InvertDiagBlocksLowerTriangular" | custom-call | tf_op jit(solution)/shard_map/jit(cholesky)/cholesky | solution.py:66
  226.8 2.0 copy-done.1
  228.7 2.4 convolution_subtract_fusion.1
  231.1 11.7 %cholesky.466 = f32[128,128]{1,0:T(8,128)S(1)} custom-call(f32[128,128]{1,0:T(8,128)S(1)} %cholesky.586), custom_call_target="Cholesky" | custom-call | tf_op jit(solution)/shard_map/jit(cholesky)/cholesky | solution.py:66
  243.6 9.8 %custom-call.64 = f32[1,128,128]{1,2,0:T(8,128)S(1)} custom-call(f32[1,128,128]{2,1,0:T(8,128)S(1)} %get-tuple-element.44), custom_call_target="InvertDiagBlocksLowerTriangular" | custom-call | tf_op jit(solution)/shard_map/jit(cholesky)/cholesky | solution.py:66
  253.4 1.3 convolution_dynamic-update-slice_fusion.1
  254.7 3.3 convolution_subtract_fusion.2
  258.1 11.7 %cholesky.485 = f32[128,128]{1,0:T(8,128)S(1)} custom-call(f32[128,128]{1,0:T(8,128)S(1)} %cholesky.591), custom_call_target="Cholesky" | custom-call | tf_op jit(solution)/shard_map/jit(cholesky)/cholesky | solution.py:66
  270.6 9.8 %custom-call.65 = f32[1,128,128]{1,2,0:T(8,128)S(1)} custom-call(f32[1,128,128]{2,1,0:T(8,128)S(1)} %get-tuple-element.42), custom_call_target="InvertDiagBlocksLowerTriangular" | custom-call | tf_op jit(solution)/shard_map/jit(cholesky)/cholesky | solution.py:66
  280.4 1.1 convolution_dynamic-update-slice_fusion.2
  281.5 3.1 convolution_subtract_fusion.3
  284.7 12.1 %cholesky.504 = f32[128,128]{1,0:T(8,128)S(1)} custom-call(f32[128,128]{1,0:T(8,128)S(1)} %cholesky.596), custom_call_target="Cholesky" | custom-call | tf_op jit(solution)/shard_map/jit(cholesky)/cholesky | solution.py:66
  297.5 9.8 %custom-call.66 = f32[1,128,128]{1,2,0:T(8,128)S(1)} custom-call(f32[1,128,128]{2,1,0:T(8,128)S(1)} %get-tuple-element.40), custom_call_target="InvertDiagBlocksLowerTriangular" | custom-call | tf_op jit(solution)/shard_map/jit(cholesky)/cholesky | solution.py:66
  307.3 1.1 convolution_dynamic-update-slice_fusion.3
  308.5 3.1 convolution_subtract_fusion.4
  311.6 11.7 %cholesky.524 = f32[128,128]{1,0:T(8,128)S(1)} custom-call(f32[128,128]{1,0:T(8,128)S(1)} %cholesky.601), custom_call_target="Cholesky" | custom-call | tf_op jit(solution)/shard_map/jit(cholesky)/cholesky | solution.py:66
  324.0 9.8 %custom-call.67 = f32[1,128,128]{1,2,0:T(8,128)S(1)} custom-call(f32[1,128,128]{2,1,0:T(8,128)S(1)} %get-tuple-element.38), custom_call_target="InvertDiagBlocksLowerTriangular" | custom-call | tf_op jit(solution)/shard_map/jit(cholesky)/cholesky | solution.py:66
  333.8 1.0 convolution_dynamic-update-slice_fusion.4
  334.8 2.8 convolution_subtract_fusion.5
  337.7 11.7 %cholesky.544 = f32[128,128]{1,0:T(8,128)S(1)} custom-call(f32[128,128]{1,0:T(8,128)S(1)} %cholesky.606), custom_call_target="Cholesky" | custom-call | tf_op jit(solution)/shard_map/jit(cholesky)/cholesky | solution.py:66
  350.2 9.8 %custom-call.68 = f32[1,128,128]{1,2,0:T(8,128)S(1)} custom-call(f32[1,128,128]{2,1,0:T(8,128)S(1)} %get-tuple-element.36), custom_call_target="InvertDiagBlocksLowerTriangular" | custom-call | tf_op jit(solution)/shard_map/jit(cholesky)/cholesky | solution.py:66
  360.0 0.9 convolution_dynamic-update-slice_fusion.5
  360.9 2.1 convolution_subtract_fusion.6
  363.0 11.7 %cholesky.562 = f32[128,128]{1,0:T(8,128)S(1)} custom-call(f32[128,128]{1,0:T(8,128)S(1)} %convolution_subtract_fusion.6), custom_call_target="Cholesky" | custom-call | tf_op jit(solution)/shard_map/jit(cholesky)/cholesky | solution.py:66
  385.2 6.7 %fusion.5 = (f32[1024,1024]{0,1:T(8,128)}, f32[1,1024,1024]{2,1,0:T(8,128)}) fusion(f32[1024,1024]{0,1:T(8,128)} %constant_dynamic-update-slice_fusion.30, pred[]{:T(512)S(6)} %cholesky.576), kind=kLoop, calls=%fused_computation.12 | loop fusion | flops 4194304 | bytes 12582913 | tf_op jit(solution)/shard_map/triangular_solve | solution.py:67
  391.9 24.1 %while.1 = (s32[]{:T(128)}, f32[1024,1024]{0,1:T(8,128)}, s32[8,2]{0,1:T(2,128)S(1)}, f32[8,128,128]{2,1,0:T(8,128)S(1)}, s32[]{:T(128)}) while((s32[]{:T(128)}, f32[1024,1024]{0,1:T(8,128)}, s32[8,2]{0,1:T(2,128)S(1)}, f32[8,128,128]{2,1,0:T(8,128)S(1)}, s32[]{:T(128)}) %tuple.59), condition=%wide.while_cond, body=%wide.while_body.sunk | while | flops 2 | bytes 393329 | solution.py:67
  392.7 2.3 dynamic-slice.7
  395.7 2.3 dynamic-slice.7
  398.7 2.3 dynamic-slice.7
  401.7 2.3 dynamic-slice.7
  404.7 2.3 dynamic-slice.7
  407.7 2.3 dynamic-slice.7
  410.7 2.3 dynamic-slice.7
  413.7 2.2 dynamic-slice.7
  416.0 78.6 %custom-call.69 = f32[8,128,128]{1,2,0:T(8,128)S(1)} custom-call(f32[8,128,128]{2,1,0:T(8,128)S(1)} %get-tuple-element.10), custom_call_target="InvertDiagBlocksLowerTriangular" | custom-call | tf_op jit(solution)/shard_map/triangular_solve | solution.py:67
  494.8 1.0 convolution_subtract_fusion.10
  496.0 1.1 convolution_subtract_fusion.9
  497.3 1.2 convolution_subtract_fusion.8
  498.6 1.2 convolution_subtract_fusion.7
  500.0 1.3 convolution_subtract_fusion.13
  501.5 1.3 convolution_subtract_fusion.12
  503.0 1.4 convolution_subtract_fusion.11
  504.7 11.0 %psum.15 = f32[32]{0:T(128)} all-reduce(f32[32]{0:T(128)S(1)} %broadcast_multiply_fusion), channel_id=1, replica_groups=mesh['rep'=32,'layer'=4] {'layer'}, use_global_device_ids=true, to_apply=%region_20.21 | all-reduce | flops 32 | bytes 256 | tf_op jit(solution)/shard_map/psum | solution.py:71
  (116 shorter events, 21.1 us)
Async XLA Ops:
  7.2 13.6 %copy-start = (bf16[1,32,8192]{2,1,0:T(8,128)(2,1)S(1)}, bf16[1,32,8192]{2,1,0:T(8,128)(2,1)}, u32[]{:S(2)}) copy-start(bf16[1,32,8192]{2,1,0:T(8,128)(2,1)} %param.9) | copy-start | bytes 1572868
  7.2 154.3 %all-reduce.3.cloned.1.call-start = ((), (), s32[]{:S(2)}) async-start(), calls=%async_computation | async-start | bytes 8388608 | tf_op jit(solution)/shard_map/psum | solution.py:63
  8.1 24.2 %collective-permute-start.1 = (f32[1]{0:T(128)S(1)}, f32[1]{0:T(128)}, u32[]{:S(2)}, u32[]{:S(2)}) collective-permute-start(f32[1]{0:T(128)S(1)} %bitcast.148), channel_id=1, source_target_pairs={{4,0},{8,4},{12,8},{16,12},{20,16},{24,20},{28,24},{32,28},{36,32}... | collective-permute-start | bytes 20 | tf_op jit(solution)/shard_map/ppermute | solution.py:13
  20.8 10.1 %copy-start.4 = (s32[512]{0:T(512)S(1)}, s32[512]{0:T(512)}, u32[]{:S(2)}) copy-start(s32[512]{0:T(512)} %param.10) | copy-start | bytes 6148
  20.8 11.5 %copy-start.5 = (s32[62]{0:T(128)S(1)}, s32[62]{0:T(128)}, u32[]{:S(2)}) copy-start(s32[62]{0:T(128)} %param.11) | copy-start | bytes 748
  27.6 6.2 %collective-permute-start = (f32[1,1024]{1,0:T(1,128)S(1)}, f32[1,1024]{1,0:T(1,128)S(1)}, u32[]{:S(2)}, u32[]{:S(2)}) collective-permute-start(f32[1,1024]{1,0:T(1,128)S(1)} %slice.248), channel_id=1, source_target_pairs={{4,0},{8,4},{12,8},{16,12},{20,16},{24,20},{28,24},{32,28},{36,32}... | collective-permute-start | bytes 12296 | tf_op jit(solution)/shard_map/ppermute | solution.py:13
  34.1 8.1 %collective-permute-start.3 = (bf16[32,1024]{1,0:T(8,128)(2,1)S(1)}, bf16[32,1024]{1,0:T(8,128)(2,1)S(1)}, u32[]{:S(2)}, u32[]{:S(2)}) collective-permute-start(bf16[32,1024]{1,0:T(8,128)(2,1)S(1)} %convolution_convert_fusion), channel_id=1, source_target_pairs={{0,4},{4,8},{8,12},{12,16},{16,20},{20,24},{24,28},{28,32},{32,36}... | collective-permute-start | bytes 196616 | tf_op jit(solution)/shard_map/ppermute | solution.py:13
  36.2 7.7 %collective-permute-start.2 = (bf16[32,1024]{1,0:T(8,128)(2,1)S(1)}, bf16[32,1024]{1,0:T(8,128)(2,1)S(1)}, u32[]{:S(2)}, u32[]{:S(2)}) collective-permute-start(bf16[32,1024]{1,0:T(8,128)(2,1)S(1)} %convolution_convert_fusion.1), channel_id=1, source_target_pairs={{4,0},{8,4},{12,8},{16,12},{20,16},{24,20},{28,24},{32,28},{36,32}... | collective-permute-start | bytes 196616 | tf_op jit(solution)/shard_map/ppermute | solution.py:13
  43.9 450.7 %copy-start.3 = (bf16[32,1024]{1,0:T(8,128)(2,1)}, bf16[32,1024]{1,0:T(8,128)(2,1)S(1)}, u32[]{:S(2)}) copy-start(bf16[32,1024]{1,0:T(8,128)(2,1)S(1)} %get-tuple-element.28) | copy-start | bytes 196612
  176.8 2.0 copy-start.2
  226.7 2.0 copy-start.1
Sparse Core Ops, SparseCore 0:
  46.9 114.5 all-reduce.2
where the time goes:
time: 530 us; the launch traced here: 523 us
  other arithmetic  267 us (50%)
  waiting for transfers between devices  116 us (22%)
  matrix products  51.9 us (10%)
  local copies, waits for them, and re-layouts  39.8 us (8%)
  between operations  19.9 us (4%)
  starting transfers between devices  16 us (3%)
  blocking collectives  11 us (2%)
    another operation x30, other arithmetic, on_device(): lower = jnp.linalg.cholesky(hessian)  168 us
    psum x1, waiting for transfers between devices, on_device(): gram = lax.psum(local_gram, 'rep')  115 us
    another operation x3, other arithmetic, on_device(): lax.linalg.triangular_solve(lower, mine.T.astype(jnp.float32), left_side=...  85.3 us
    another operation x14, matrix products, on_device(): lower = jnp.linalg.cholesky(hessian)  25.9 us
    another operation x40, local copies, waits for them, and re-layouts  23.6 us
    ppermute x4, starting transfers between devices, shifted(): return lax.ppermute(block, axis, route)  15.9 us
    psum x1, blocking collectives, on_device(): influence = lax.psum(quad, 'layer')  11 us
  transfers between devices with their start and end apart: 5, of which 2 were waited for; matrix products, arithmetic and copies ran while one was open for 3% of the time, Pallas kernels for 0%

commit v1 on v0

--- a/solution.py
+++ b/solution.py
@@ -60,7 +60,11 @@
     ).astype(jnp.bfloat16)
     rows_contract = (((0,), (0,)), ((), ()))
     local_gram = lax.dot_general(mine, mine, rows_contract, preferred_element_type=jnp.float32)
-    gram = lax.psum(local_gram, "rep")
+    size = lax.axis_size("rep")
+    gram, stride = (local_gram, 1)
+    while stride < size:
+        gram = gram + lax.ppermute(gram, "rep", [(i_2, i_2 ^ stride) for i_2 in range(size)])
+        stride = 2 * stride
     total_docs = BAL * n_rep
     hessian = gram / total_docs + DAMPING * jnp.eye(width, dtype=jnp.float32)
     lower = jnp.linalg.cholesky(hessian)

time: 530 us -> 789 us (1.49)
  waiting for transfers between devices: 116 us -> 375 us
  between operations: 19.9 us -> 6.55 us
  other arithmetic: 267 us -> 276 us
    ppermute x0 -> x5, waiting for transfers between devices: none -> 373 us  [on_device(): lax.ppermute(gram, 'rep', [(i_2, i_2 ^ stride) for i_2 in range(size)])]
    psum x1 -> x0, waiting for transfers between devices: 115 us -> none  [on_device(): gram = lax.psum(local_gram, 'rep')]
  transfers between devices with their start and end apart: 5 -> 9, of which waited for: 2 -> 6; matrix products, arithmetic and copies ran while one was open for 3% -> 2% of each run, Pallas kernels for 0% -> 0%
where the time goes in v1:
time: 789 us; the launch traced here: 779 us
  waiting for transfers between devices  375 us (48%)
  other arithmetic  276 us (35%)
  matrix products  50 us (6%)
  local copies, waits for them, and re-layouts  39.2 us (5%)
  starting transfers between devices  20.5 us (3%)
  blocking collectives  11.3 us (1%)
    ppermute x5, waiting for transfers between devices, on_device(): lax.ppermute(gram, 'rep', [(i_2, i_2 ^ stride) for i_2 in range(size)])  373 us
    another operation x30, other arithmetic, on_device(): lower = jnp.linalg.cholesky(hessian)  168 us
    another operation x3, other arithmetic, on_device(): lax.linalg.triangular_solve(lower, mine.T.astype(jnp.float32), left_side=...  85.3 us
    another operation x14, matrix products, on_device(): lower = jnp.linalg.cholesky(hessian)  26.1 us
    another operation x40, local copies, waits for them, and re-layouts  23.6 us
    ppermute x4, starting transfers between devices, shifted(): return lax.ppermute(block, axis, route)  15.9 us
  transfers between devices with their start and end apart: 9, of which 6 were waited for; matrix products, arithmetic and copies ran while one was open for 2% of the time, Pallas kernels for 0%

profile of v1, /device:TPU:6, one launch (start us, length us, event | category | flops | bytes accessed | tf_op | source)
XLA Modules:
  0.0 779.3 jit_solution(8234833383597549288)
XLA Ops:
  1.6 5.7 collective-permute-start.1
  8.0 6.2 fusion.10
  14.2 6.7 fusion.7
  21.0 2.6 collective-permute-start
  25.8 1.4 maximum_sqrt_fusion
  27.6 1.9 collective-permute-start.3
  29.7 5.8 collective-permute-start.2
  35.7 1.7 collective-permute-done.2
  38.2 7.1 collective-permute-done.4
  45.4 1.4 add.125
  46.8 92.6 %collective-permute-done.5 = f32[1024,1024]{0,1:T(8,128)S(1)} collective-permute-done((f32[1024,1024]{0,1:T(8,128)S(1)}, f32[1024,1024]{0,1:T(8,128)S(1)}, u32[]{:S(2)}, u32[]{:S(2)}) %collective-permute-start.5) | collective-permute-done | bytes 4194336 | tf_op jit(solution)/shard_map/ppermute | solution.py:66
  139.4 1.4 add.126
  140.9 93.3 %collective-permute-done.6 = f32[1024,1024]{0,1:T(8,128)S(1)} collective-permute-done((f32[1024,1024]{0,1:T(8,128)S(1)}, f32[1024,1024]{0,1:T(8,128)S(1)}, u32[]{:S(2)}, u32[]{:S(2)}) %collective-permute-start.6) | collective-permute-done | bytes 4194336 | tf_op jit(solution)/shard_map/ppermute | solution.py:66
  234.2 1.4 add.127
  235.5 1.9 collective-permute-start.7
  237.5 90.0 %collective-permute-done.7 = f32[1024,1024]{0,1:T(8,128)S(1)} collective-permute-done((f32[1024,1024]{0,1:T(8,128)S(1)}, f32[1024,1024]{0,1:T(8,128)S(1)}, u32[]{:S(2)}, u32[]{:S(2)}) %collective-permute-start.7) | collective-permute-done | bytes 4194336 | tf_op jit(solution)/shard_map/ppermute | solution.py:66
  327.5 2.9 add.128
  330.4 2.3 collective-permute-start.8
  332.7 90.2 %collective-permute-done.8 = f32[1024,1024]{0,1:T(8,128)} collective-permute-done((f32[1024,1024]{0,1:T(8,128)}, f32[1024,1024]{0,1:T(8,128)}, u32[]{:S(2)}, u32[]{:S(2)}) %collective-permute-start.8) | collective-permute-done | bytes 4194336 | tf_op jit(solution)/shard_map/ppermute | solution.py:66
  422.9 6.9 select_add_fusion
  429.9 5.3 copy.31
  435.2 4.4 fusion.4
  439.7 2.0 copy-done.3
  441.7 11.7 %cholesky.222 = f32[128,128]{1,0:T(8,128)S(1)} custom-call(f32[128,128]{1,0:T(8,128)S(1)} %cholesky.577), custom_call_target="Cholesky" | custom-call | tf_op jit(solution)/shard_map/jit(cholesky)/cholesky | solution.py:70
  453.6 9.8 %custom-call.62 = f32[1,128,128]{1,2,0:T(8,128)S(1)} custom-call(f32[1,128,128]{2,1,0:T(8,128)S(1)} %get-tuple-element.48), custom_call_target="InvertDiagBlocksLowerTriangular" | custom-call | tf_op jit(solution)/shard_map/jit(cholesky)/cholesky | solution.py:70
  463.4 1.5 fusion.41
  465.1 1.6 slice_subtract_fusion
  466.7 11.7 %cholesky.243 = f32[128,128]{1,0:T(8,128)S(1)} custom-call(f32[128,128]{1,0:T(8,128)S(1)} %cholesky.581), custom_call_target="Cholesky" | custom-call | tf_op jit(solution)/shard_map/jit(cholesky)/cholesky | solution.py:70
  478.9 9.8 %custom-call.63 = f32[1,128,128]{1,2,0:T(8,128)S(1)} custom-call(f32[1,128,128]{2,1,0:T(8,128)S(1)} %get-tuple-element.46), custom_call_target="InvertDiagBlocksLowerTriangular" | custom-call | tf_op jit(solution)/shard_map/jit(cholesky)/cholesky | solution.py:70
  489.9 2.0 copy-done.2
  491.8 2.4 slice_subtract_fusion.1
  494.3 11.7 %cholesky.466 = f32[128,128]{1,0:T(8,128)S(1)} custom-call(f32[128,128]{1,0:T(8,128)S(1)} %cholesky.586), custom_call_target="Cholesky" | custom-call | tf_op jit(solution)/shard_map/jit(cholesky)/cholesky | solution.py:70
  506.7 9.8 %custom-call.64 = f32[1,128,128]{1,2,0:T(8,128)S(1)} custom-call(f32[1,128,128]{2,1,0:T(8,128)S(1)} %get-tuple-element.44), custom_call_target="InvertDiagBlocksLowerTriangular" | custom-call | tf_op jit(solution)/shard_map/jit(cholesky)/cholesky | solution.py:70
  516.6 1.3 convolution_dynamic-update-slice_fusion.1
  517.8 3.3 slice_subtract_fusion.2
  521.1 11.7 %cholesky.485 = f32[128,128]{1,0:T(8,128)S(1)} custom-call(f32[128,128]{1,0:T(8,128)S(1)} %cholesky.591), custom_call_target="Cholesky" | custom-call | tf_op jit(solution)/shard_map/jit(cholesky)/cholesky | solution.py:70
  533.6 9.8 %custom-call.65 = f32[1,128,128]{1,2,0:T(8,128)S(1)} custom-call(f32[1,128,128]{2,1,0:T(8,128)S(1)} %get-tuple-element.42), custom_call_target="InvertDiagBlocksLowerTriangular" | custom-call | tf_op jit(solution)/shard_map/jit(cholesky)/cholesky | solution.py:70
  544.6 3.1 slice_subtract_fusion.3
  547.7 11.9 %cholesky.504 = f32[128,128]{1,0:T(8,128)S(1)} custom-call(f32[128,128]{1,0:T(8,128)S(1)} %cholesky.596), custom_call_target="Cholesky" | custom-call | tf_op jit(solution)/shard_map/jit(cholesky)/cholesky | solution.py:70
  560.4 9.8 %custom-call.66 = f32[1,128,128]{1,2,0:T(8,128)S(1)} custom-call(f32[1,128,128]{2,1,0:T(8,128)S(1)} %get-tuple-element.40), custom_call_target="InvertDiagBlocksLowerTriangular" | custom-call | tf_op jit(solution)/shard_map/jit(cholesky)/cholesky | solution.py:70
  571.3 3.1 slice_subtract_fusion.4
  574.4 11.7 %cholesky.524 = f32[128,128]{1,0:T(8,128)S(1)} custom-call(f32[128,128]{1,0:T(8,128)S(1)} %cholesky.601), custom_call_target="Cholesky" | custom-call | tf_op jit(solution)/shard_map/jit(cholesky)/cholesky | solution.py:70
  586.9 9.8 %custom-call.67 = f32[1,128,128]{1,2,0:T(8,128)S(1)} custom-call(f32[1,128,128]{2,1,0:T(8,128)S(1)} %get-tuple-element.38), custom_call_target="InvertDiagBlocksLowerTriangular" | custom-call | tf_op jit(solution)/shard_map/jit(cholesky)/cholesky | solution.py:70
  597.7 3.1 slice_subtract_fusion.5
  600.8 11.7 %cholesky.544 = f32[128,128]{1,0:T(8,128)S(1)} custom-call(f32[128,128]{1,0:T(8,128)S(1)} %cholesky.606), custom_call_target="Cholesky" | custom-call | tf_op jit(solution)/shard_map/jit(cholesky)/cholesky | solution.py:70
  613.3 9.8 %custom-call.68 = f32[1,128,128]{1,2,0:T(8,128)S(1)} custom-call(f32[1,128,128]{2,1,0:T(8,128)S(1)} %get-tuple-element.36), custom_call_target="InvertDiagBlocksLowerTriangular" | custom-call | tf_op jit(solution)/shard_map/jit(cholesky)/cholesky | solution.py:70
  624.0 2.1 slice_subtract_fusion.6
  626.1 11.7 %cholesky.562 = f32[128,128]{1,0:T(8,128)S(1)} custom-call(f32[128,128]{1,0:T(8,128)S(1)} %slice_subtract_fusion.6), custom_call_target="Cholesky" | custom-call | tf_op jit(solution)/shard_map/jit(cholesky)/cholesky | solution.py:70
  648.3 6.7 fusion.5
  655.1 24.0 %while.1 = (s32[]{:T(128)}, f32[1024,1024]{0,1:T(8,128)}, s32[8,2]{0,1:T(2,128)S(1)}, f32[8,128,128]{2,1,0:T(8,128)S(1)}, s32[]{:T(128)}) while((s32[]{:T(128)}, f32[1024,1024]{0,1:T(8,128)}, s32[8,2]{0,1:T(2,128)S(1)}, f32[8,128,128]{2,1,0:T(8,128)S(1)}, s32[]{:T(128)}) %tuple.59), condition=%wide.while_cond, body=%wide.while_body.sunk | while | flops 2 | bytes 393329 | solution.py:71
  655.8 2.3 dynamic-slice.7
  658.8 2.3 dynamic-slice.7
  661.8 2.3 dynamic-slice.7
  664.8 2.3 dynamic-slice.7
  667.8 2.3 dynamic-slice.7
  670.8 2.3 dynamic-slice.7
  673.8 2.3 dynamic-slice.7
  676.8 2.2 dynamic-slice.7
  679.1 78.6 %custom-call.69 = f32[8,128,128]{1,2,0:T(8,128)S(1)} custom-call(f32[8,128,128]{2,1,0:T(8,128)S(1)} %get-tuple-element.10), custom_call_target="InvertDiagBlocksLowerTriangular" | custom-call | tf_op jit(solution)/shard_map/triangular_solve | solution.py:71
  761.7 1.2 convolution_subtract_fusion
  763.1 1.3 convolution_subtract_fusion.6
  764.6 1.3 convolution_subtract_fusion.5
  766.1 1.4 convolution_subtract_fusion.4
  767.8 11.3 %psum.7 = f32[32]{0:T(128)} all-reduce(f32[32]{0:T(128)S(1)} %broadcast_multiply_fusion), channel_id=1, replica_groups=mesh['rep'=32,'layer'=4] {'layer'}, use_global_device_ids=true, to_apply=%region_19.20 | all-reduce | flops 32 | bytes 256 | tf_op jit(solution)/shard_map/psum | solution.py:75
  (129 shorter events, 31.4 us)
Async XLA Ops:
  0.6 13.6 %copy-start = (bf16[1,32,8192]{2,1,0:T(8,128)(2,1)S(1)}, bf16[1,32,8192]{2,1,0:T(8,128)(2,1)}, u32[]{:S(2)}) copy-start(bf16[1,32,8192]{2,1,0:T(8,128)(2,1)} %param.9) | copy-start | bytes 1572868
  1.6 24.2 %collective-permute-start.1 = (f32[1]{0:T(128)S(1)}, f32[1]{0:T(128)}, u32[]{:S(2)}, u32[]{:S(2)}) collective-permute-start(f32[1]{0:T(128)S(1)} %bitcast.148), channel_id=1, source_target_pairs={{4,0},{8,4},{12,8},{16,12},{20,16},{24,20},{28,24},{32,28},{36,32}... | collective-permute-start | bytes 20 | tf_op jit(solution)/shard_map/ppermute | solution.py:13
  14.2 10.1 %copy-start.5 = (s32[512]{0:T(512)S(1)}, s32[512]{0:T(512)}, u32[]{:S(2)}) copy-start(s32[512]{0:T(512)} %param.10) | copy-start | bytes 6148
  14.2 11.5 %copy-start.6 = (s32[62]{0:T(128)S(1)}, s32[62]{0:T(128)}, u32[]{:S(2)}) copy-start(s32[62]{0:T(128)} %param.11) | copy-start | bytes 748
  21.0 6.2 collective-permute-start
  27.6 8.1 %collective-permute-start.3 = (bf16[32,1024]{1,0:T(8,128)(2,1)S(1)}, bf16[32,1024]{1,0:T(8,128)(2,1)S(1)}, u32[]{:S(2)}, u32[]{:S(2)}) collective-permute-start(bf16[32,1024]{1,0:T(8,128)(2,1)S(1)} %convolution_convert_fusion), channel_id=1, source_target_pairs={{0,4},{4,8},{8,12},{12,16},{16,20},{20,24},{24,28},{28,32},{32,36}... | collective-permute-start | bytes 196616 | tf_op jit(solution)/shard_map/ppermute | solution.py:13
  29.7 7.7 collective-permute-start.2
  37.4 720.3 %copy-start.4 = (bf16[32,1024]{1,0:T(8,128)(2,1)}, bf16[32,1024]{1,0:T(8,128)(2,1)S(1)}, u32[]{:S(2)}) copy-start(bf16[32,1024]{1,0:T(8,128)(2,1)S(1)} %get-tuple-element.28) | copy-start | bytes 196612
  38.1 7.2 collective-permute-start.4
  46.7 92.7 %collective-permute-start.5 = (f32[1024,1024]{0,1:T(8,128)S(1)}, f32[1024,1024]{0,1:T(8,128)S(1)}, u32[]{:S(2)}, u32[]{:S(2)}) collective-permute-start(f32[1024,1024]{0,1:T(8,128)S(1)} %add.125), channel_id=1, source_target_pairs={{0,8},{4,12},{8,0},{12,4},{16,24},{20,28},{24,16},{28,20},{32,40},... | collective-permute-start | bytes 12582920 | tf_op jit(solution)/shard_map/ppermute | solution.py:66
  140.8 93.4 %collective-permute-start.6 = (f32[1024,1024]{0,1:T(8,128)S(1)}, f32[1024,1024]{0,1:T(8,128)S(1)}, u32[]{:S(2)}, u32[]{:S(2)}) collective-permute-start(f32[1024,1024]{0,1:T(8,128)S(1)} %add.126), channel_id=1, source_target_pairs={{0,16},{4,20},{8,24},{12,28},{16,0},{20,4},{24,8},{28,12},{32,48},... | collective-permute-start | bytes 12582920 | tf_op jit(solution)/shard_map/ppermute | solution.py:66
  235.5 91.9 %collective-permute-start.7 = (f32[1024,1024]{0,1:T(8,128)S(1)}, f32[1024,1024]{0,1:T(8,128)S(1)}, u32[]{:S(2)}, u32[]{:S(2)}) collective-permute-start(f32[1024,1024]{0,1:T(8,128)S(1)} %add.127), channel_id=1, source_target_pairs={{0,32},{4,36},{8,40},{12,44},{16,48},{20,52},{24,56},{28,60},{32,0... | collective-permute-start | bytes 12582920 | tf_op jit(solution)/shard_map/ppermute | solution.py:66
  330.4 92.6 %collective-permute-start.8 = (f32[1024,1024]{0,1:T(8,128)}, f32[1024,1024]{0,1:T(8,128)}, u32[]{:S(2)}, u32[]{:S(2)}) collective-permute-start(f32[1024,1024]{0,1:T(8,128)} %add.128), channel_id=1, source_target_pairs={{0,64},{4,68},{8,72},{12,76},{16,80},{20,84},{24,88},{28,92},{32,9... | collective-permute-start | bytes 12582920 | tf_op jit(solution)/shard_map/ppermute | solution.py:66
  439.7 2.0 copy-start.3
  489.9 2.0 copy-start.2
  648.3 130.8 %copy-start.1 = (bf16[1,32,8192]{2,1,0:T(8,128)(2,1)S(1)}, bf16[1,32,8192]{2,1,0:T(8,128)(2,1)}, u32[]{:S(2)}) copy-start(bf16[1,32,8192]{2,1,0:T(8,128)(2,1)} %param.9) | copy-start | bytes 1572868
